TPU v7x, 32 devices: a whole 2x2x4 slice. The times are simulated.
32 devices in a mesh: dp: 8 (over z, x), head: 4 (over y, core).
Axes of the slice: x: 2, y: 2, z: 4, core: 2. Of those that a mesh axis runs over, the one named last changes fastest.
Arguments:
- vit_ctx: bfloat16 [1024, 1536], P('dp', 'head'), may hold values from -6 to 6
- vit_resid: bfloat16 [1024, 1600], P('dp'), may hold values from -6 to 6
- vit_proj: bfloat16 [4, 384, 1600], P('head', 'dp'), may hold values from -0.15625 to 0.15625
- vit_grad: bfloat16 [1024, 1600], P('dp'), may hold values from -6 to 6
- norm_gain: float32 [1600], replicated, may hold values from 0.1 to 1.9
- cross_q: bfloat16 [96, 2048], P(None, 'head'), may hold values from -400 to 400
- key_w: bfloat16 [1600, 2048], P(None, 'head'), may hold values from -0.15625 to 0.15625
- value_w: bfloat16 [1600, 2048], P(None, 'head'), may hold values from -0.15625 to 0.15625
- out_w: bfloat16 [2048, 4096], P('head'), may hold values from -0.125 to 0.125
- query_state: bfloat16 [96, 4096], P(None, 'head'), may hold values from -1.5 to 1.5
Outputs:
- ctx_grad: bfloat16 [1024, 1536], P('dp', 'head')
- proj_grad: float32 [4, 384, 1600], P('head', 'dp')
- cross_out: bfloat16 [8, 96, 4096], P('dp', None, 'head')
All inputs are finite; a program needn't handle non-finite values.
Results may differ from a plain program's by a relative error of at most 0.017.
The roundings to bfloat16 on the way count: a program that leaves them out, or rounds other values in their place, can miss the bound.
Values may be sent and summed in bfloat16 or wider, within the bound.
A program may use at most 64 MiB of HBM per device.

v0:
```python
import math

import jax
import jax.numpy as jnp
from jax import lax
from jax.sharding import PartitionSpec as P

HD = 128


EPSILON = 1e-06


def on_device(
    vit_ctx, vit_resid, vit_proj, vit_grad, norm_gain, cross_q, key_w, value_w, out_w, query_state
):
    contract_cols = (((1,), (1,)), ((), ()))
    ctx_part = vit_ctx
    partial_value = jnp.dot(
        ctx_part,
        lax.all_gather(vit_proj, "dp", axis=1, tiled=True)[0],
        preferred_element_type=jnp.float32,
    )
    ctx_grad = lax.dot_general(
        vit_grad,
        lax.all_gather(vit_proj, "dp", axis=1, tiled=True)[0],
        contract_cols,
        preferred_element_type=jnp.float32,
    ).astype(jnp.bfloat16)
    ctx_part = vit_ctx
    grad_share = lax.psum_scatter(
        lax.dot_general(
            ctx_part, vit_grad, (((0,), (0,)), ((), ())), preferred_element_type=jnp.float32
        ),
        "dp",
        scatter_dimension=0,
        tiled=True,
    )
    proj_grad = grad_share[None]
    feature_count = partial_value.shape[1]
    summed = lax.psum(partial_value, "head")
    hidden = vit_resid.astype(jnp.float32) + summed
    row_mean = jnp.sum(hidden, axis=1, keepdims=True) / feature_count
    square_mean = jnp.sum(hidden * hidden, axis=1, keepdims=True) / feature_count
    variance = square_mean - row_mean * row_mean
    features = ((hidden - row_mean) * lax.rsqrt(variance + EPSILON) * norm_gain).astype(
        jnp.bfloat16
    )
    head_count = key_w.shape[1] // HD
    query_count = cross_q.shape[0]
    key_rows = jnp.dot(features, key_w, preferred_element_type=jnp.float32).astype(jnp.bfloat16)
    value_rows = jnp.dot(features, value_w, preferred_element_type=jnp.float32).astype(jnp.bfloat16)
    queries = cross_q.reshape(query_count, head_count, HD)
    key_heads = key_rows.reshape(-1, head_count, HD)
    value_heads = value_rows.reshape(-1, head_count, HD)
    score_scale = 1.0 / math.sqrt(HD)
    scores = (
        jnp.einsum("qhd,khd->hqk", queries, key_heads, preferred_element_type=jnp.float32)
        * score_scale
    )
    row_max = jnp.max(scores, axis=2, keepdims=True)
    exponent = jnp.exp(scores - row_max)
    attn_probs = (exponent / jnp.sum(exponent, axis=2, keepdims=True)).astype(jnp.bfloat16)
    attended = jnp.einsum(
        "hqk,khd->qhd", attn_probs, value_heads, preferred_element_type=jnp.float32
    )
    attended = attended.astype(jnp.bfloat16).reshape(query_count, head_count * HD)
    out_partial = jnp.dot(attended, out_w, preferred_element_type=jnp.float32)
    out_share = lax.psum_scatter(
        out_partial.astype(jnp.bfloat16), "head", scatter_dimension=1, tiled=True
    ).astype(jnp.float32)
    cross_out = (out_share + query_state.astype(jnp.float32)).astype(jnp.bfloat16)[None]
    return (ctx_grad, proj_grad, cross_out)


def solution(mesh):
    return jax.shard_map(
        on_device,
        mesh=mesh,
        in_specs=(
            P("dp", "head"),
            P("dp", None),
            P("head", "dp", None),
            P("dp", None),
            P(),
            P(None, "head"),
            P(None, "head"),
            P(None, "head"),
            P("head", None),
            P(None, "head"),
        ),
        out_specs=(P("dp", "head"), P("head", "dp", None), P("dp", None, "head")),
        check_vma=False,
    )
```

profile of v0, /device:TPU:0, one launch (start us, length us, event | category | flops | bytes accessed | tf_op | source)
XLA Modules:
  0.0 205.2 jit_solution(9115707101834075549)
XLA Ops:
  7.2 0.0 copy-start
  7.2 0.0 all-gather.2.cloned.1.call-start
  7.2 0.7 all-gather.2.cloned.1.call-update
  7.9 0.0 copy-start.9
  7.9 0.0 all-reduce.2.cloned.1.call-start
  8.0 46.6 %all-gather.2.cloned.1.call-done = bf16[1,384,1600]{2,1,0:T(8,128)(2,1)} async-done(((bf16[1,48,1600]{2,1,0:T(8,128)(2,1)}), bf16[1,384,1600]{2,1,0:T(8,128)(2,1)}) %all-gather.2.cloned.1.call-update) | async-done | bytes 1228816 | tf_op jit(solution)/shard_map/all_gather | solution.py:26
  54.6 2.9 %fusion.1 = f32[128,1600]{0,1:T(8,128)} fusion(bf16[128,384]{1,0:T(8,128)(2,1)} %param.10, bf16[1,384,1600]{2,1,0:T(8,128)(2,1)} %all-gather.2.cloned.1.call-done), kind=kOutput, calls=%fused_computation.2 | convolution fusion | flops 157286400 | bytes 2146304 | tf_op jit(solution)/shard_map/dot_general | solution.py:19
  57.5 0.0 all-reduce.2.cloned.1.call-update
  57.5 0.0 reduce-scatter.5.cloned.1.call-start
  57.6 34.2 %all-reduce.2.cloned.1.call-done = f32[128,1600]{0,1:T(8,128)} async-done(((f32[128,1600]{0,1:T(8,128)}), f32[128,1600]{0,1:T(8,128)}) %all-reduce.2.cloned.1.call-update) | async-done | bytes 819216 | tf_op jit(solution)/shard_map/psum | solution.py:41
  91.8 0.0 copy-done.5
  91.8 1.4 fusion.14
  93.3 0.0 copy-start.4
  93.3 0.3 multiply_convert_fusion
  93.6 0.0 copy-start.8
  93.6 0.4 fusion.12
  94.1 0.7 copy-done.4
  94.7 0.4 fusion.11
  95.2 0.2 fusion.6
  95.4 0.2 fusion.26
  95.6 0.7 fusion.13
  96.4 0.0 copy-start.6
  96.4 3.9 %convolution_convert_fusion = bf16[96,4096]{1,0:T(8,128)(2,1)} fusion(bf16[512,4096]{1,0:T(8,128)(2,1)} %param.18, bf16[4,12,8,128]{3,2,1,0:T(8,128)(2,1)S(1)} %fusion.13), kind=kOutput, calls=%fused_computation.1 | convolution fusion | flops 403046400 | bytes 5079040 | tf_op jit(solution)/shard_map/dot_general | solution.py:68
  100.3 0.0 reduce-scatter.5.cloned.1.call-update
  100.3 0.0 reduce-scatter.3.cloned.1.call-start
  100.4 2.0 fusion.27
  102.4 0.0 reduce-scatter.3.cloned.1.call-update
  102.4 1.3 copy-done.1
  103.7 1.2 fusion.8
  104.8 18.8 %reduce-scatter.5.cloned.1.call-done = bf16[96,1024]{1,0:T(8,128)(2,1)} async-done(((bf16[96,4096]{1,0:T(8,128)(2,1)}), bf16[96,1024]{1,0:T(8,128)(2,1)}) %reduce-scatter.5.cloned.1.call-update) | async-done | bytes 196624 | tf_op jit(solution)/shard_map/reduce_scatter | solution.py:69
  123.7 1.7 fusion.15
  125.3 73.4 %reduce-scatter.3.cloned.1.call-done = f32[48,1600]{1,0:T(8,128)} async-done(((f32[384,1600]{1,0:T(8,128)}), f32[48,1600]{1,0:T(8,128)}) %reduce-scatter.3.cloned.1.call-update) | async-done | bytes 307216 | tf_op jit(solution)/shard_map/reduce_scatter | solution.py:31
  (13 shorter events, 0.0 us)
Async XLA Ops:
  7.2 86.4 %copy-start = (bf16[1600,512]{1,0:T(8,128)(2,1)S(1)}, bf16[1600,512]{1,0:T(8,128)(2,1)}, u32[]{:S(2)}) copy-start(bf16[1600,512]{1,0:T(8,128)(2,1)} %param.16) | copy-start | bytes 4915204
  7.2 84.6 %copy-start.5 = (bf16[128,1600]{0,1:T(8,128)(2,1)S(1)}, bf16[128,1600]{0,1:T(8,128)(2,1)}, u32[]{:S(2)}) copy-start(bf16[128,1600]{0,1:T(8,128)(2,1)} %param.11) | copy-start | bytes 1228804
  7.2 47.4 %all-gather.2.cloned.1.call-start = ((), (), s32[]{:S(2)}) async-start(), calls=%async_computation.2 | async-start | bytes 1437696 | tf_op jit(solution)/shard_map/all_gather | solution.py:26
  7.9 85.3 %copy-start.9 = (f32[1600]{0:T(1024)S(1)}, f32[1600]{0:T(1024)}, u32[]{:S(2)}) copy-start(f32[1600]{0:T(1024)} %param.14) | copy-start | bytes 19204
  7.9 83.9 %all-reduce.2.cloned.1.call-start = ((), (), s32[]{:S(2)}) async-start(), calls=%async_computation.4 | async-start | bytes 1638400 | tf_op jit(solution)/shard_map/psum | solution.py:41
  57.5 66.1 %reduce-scatter.5.cloned.1.call-start = ((), (), s32[]{:S(2)}) async-start(), calls=%async_computation.5 | async-start | bytes 983040 | tf_op jit(solution)/shard_map/reduce_scatter | solution.py:69
  91.8 1.5 copy-start.2
  93.3 1.4 copy-start.4
  93.6 1.6 copy-start.8
  96.4 4.0 %copy-start.3 = (bf16[128,1600]{0,1:T(8,128)(2,1)S(1)}, bf16[128,1600]{0,1:T(8,128)(2,1)}, u32[]{:S(2)}) copy-start(bf16[128,1600]{0,1:T(8,128)(2,1)} %param.13) | copy-start | bytes 1228804
  96.4 4.0 %copy-start.6 = (bf16[128,384]{1,0:T(8,128)(2,1)S(1)}, bf16[128,384]{1,0:T(8,128)(2,1)}, u32[]{:S(2)}) copy-start(bf16[128,384]{1,0:T(8,128)(2,1)} %param.10) | copy-start | bytes 294916
  100.3 98.4 %reduce-scatter.3.cloned.1.call-start = ((), (), s32[]{:S(2)}) async-start(), calls=%async_computation.3 | async-start | bytes 2875392 | tf_op jit(solution)/shard_map/reduce_scatter | solution.py:31
  102.4 1.3 copy-start.1
  102.4 21.3 %copy-start.7 = (bf16[96,1024]{1,0:T(8,128)(2,1)S(1)}, bf16[96,1024]{1,0:T(8,128)(2,1)}, u32[]{:S(2)}) copy-start(bf16[96,1024]{1,0:T(8,128)(2,1)} %param.19) | copy-start | bytes 589828
Sparse Core Ops, SparseCore 0:
  10.2 44.4 all-gather.1
  57.7 34.0 all-reduce.1
  100.4 23.1 reduce-scatter.4
  127.6 71.0 reduce-scatter.2
where the time goes:
time: 205 us
  waiting for transfers between devices  174 us (85%)
  between operations  13.9 us (7%)
  matrix products  11.8 us (6%)
  other arithmetic  3.64 us (2%)
    reduce_scatter x1, waiting for transfers between devices, on_device(): lax.psum_scatter(lax.dot_general(ctx_part, vit_grad, (((0,), (0,)), ((),...  73.4 us
    all_gather x1, waiting for transfers between devices, on_device(): lax.all_gather(vit_proj, 'dp', axis=1, tiled=True)[0]  46.6 us
    psum x1, waiting for transfers between devices, on_device(): summed = lax.psum(partial_value, 'head')  34.2 us
    reduce_scatter x1, waiting for transfers between devices, on_device(): lax.psum_scatter(out_partial.astype(jnp.bfloat16), 'head', scatter_dimens...  18.8 us
  transfers between devices with their start and end apart: 4, of which 4 were waited for; matrix products, arithmetic and copies ran while one was open for 2% of the time, Pallas kernels for 0%

commit v1 on v0

v1 whole, which is shorter than its diff:
```python
import functools
import math

import jax
import jax.numpy as jnp
from jax import lax
from jax.experimental import pallas as pl
from jax.experimental.pallas import tpu as pltpu
from jax.sharding import PartitionSpec as P

HD = 128
EPSILON = 1e-06
MESH = pl.DeviceIdType.MESH
F32 = jnp.float32
BF16 = jnp.bfloat16


def peer_along(at, step, count):
    if count & (count - 1):
        return lax.rem(at + step, count)
    bit = 1
    while bit < count:
        if step & bit:
            at = at + bit - 2 * bit * lax.rem(at // bit, 2)
        bit *= 2
    return at


def kernel(names, n, h, fused, *refs):
    r = dict(zip(names, refs))
    ctx, resid, proj, grad, gain, cross_q, query_state = (
        r[k] for k in ("ctx", "resid", "proj", "grad", "gain", "cross_q", "query_state")
    )
    d, e = lax.axis_index("dp"), lax.axis_index("head")
    m, chips = n // 2, h // 2
    z, x = d // 2, lax.rem(d, 2)
    y, c = e // 2, lax.rem(e, 2)
    x_peer = (2 * z + 1 - x, e)
    z_pos = [z] + [peer_along(z, k, m) for k in range(1, m)] if fused else []
    z_peer = [(2 * p + x, e) for p in z_pos]
    core_peer = (d, 2 * y + 1 - c)
    y_pos = [y] + [lax.rem(y + k, chips) for k in range(1, chips)]
    y_peer = [(d, 2 * p + c) for p in y_pos]

    def remote(src, dst, name, at, device):
        copy = pltpu.make_async_remote_copy(
            src_ref=src,
            dst_ref=dst,
            send_sem=r[name + "_s"].at[at],
            recv_sem=r[name + "_r"].at[at],
            device_id=device,
            device_id_type=MESH,
        )
        copy.start()
        return copy

    loads = []
    for i, name in enumerate(("key_w", "value_w", "out_w")):
        load = pltpu.make_async_copy(r[name], r[name + "_v"], r["load"].at[i])
        load.start()
        loads.append(load)

    greet = ([x_peer] + z_peer[1:] if fused else []) + [core_peer] + y_peer[1:]
    barrier = pltpu.get_barrier_semaphore()
    for device in greet:
        pl.semaphore_signal(barrier, inc=1, device_id=device, device_id_type=MESH)
    pl.semaphore_wait(barrier, len(greet))

    if fused:
        rows = proj.shape[0]
        width = proj.shape[1]
        gath, dwf, dwb = r["gath"], r["dwf"], r["dwb"]
        ag_z = [None] + [remote(proj, gath.at[d], "ag_z", k - 1, z_peer[k]) for k in range(1, m)]
        ag_x = [remote(proj, gath.at[d], "ag_x", 0, x_peer)]
        gath[d] = proj[...]
        ctx_t = ctx[...].T
        for lo in range(0, width, 256):
            hi = min(lo + 256, width)
            part = jnp.dot(ctx_t, grad[:, lo:hi], preferred_element_type=F32)
            dwf[:, :, lo:hi] = part.reshape(n, rows, hi - lo)
        for k in range(m):
            dwb[k] = dwf[2 * z_pos[k] + 1 - x].astype(BF16)
        for k in range(1, m):
            ag_z[k].wait_recv()
            owner = 2 * z_pos[k] + x
            ag_x.append(remote(gath.at[owner], gath.at[owner], "ag_x", k, x_peer))
        rs_x = {}
        for k in list(range(m - 1, 0, -1)) + [0]:
            rs_x[k] = remote(dwb.at[k], r["xrecv"].at[k], "rs_x", k, x_peer)
        rs_z = {}

        def pass_on(k):
            rs_x[k].wait_recv()
            r["zsend"][k - 1] = (dwf[2 * z_pos[k] + x] + r["xrecv"][k].astype(F32)).astype(BF16)
            rs_z[k] = remote(r["zsend"].at[k - 1], r["zrecv"].at[k - 1], "rs_z", k - 1, z_peer[k])

        for k in range(m):
            ag_x[k].wait_recv()
        matrix = gath[...].reshape(n * rows, width)
        todo = list(range(m - 1, 0, -1))
    else:
        matrix = proj[...]
        todo = []

    half = ctx.shape[0] // 2
    own_rows = pl.ds(pl.multiple_of(c * half, half), half)
    peer_rows = pl.ds(pl.multiple_of((1 - c) * half, half), half)
    hs, feat = r["hs"], r["feat"]
    hs[1] = jnp.dot(ctx[peer_rows, :], matrix, preferred_element_type=F32)
    to_core = remote(hs.at[1], r["crecv"], "core", 0, core_peer)
    hs[0] = jnp.dot(ctx[own_rows, :], matrix, preferred_element_type=F32)
    to_core.wait_recv()
    chip_sum = hs[0] + r["crecv"][...]
    hs[0] = chip_sum
    r["ysend"][...] = chip_sum.astype(BF16)
    to_y = [remote(r["ysend"], r["yrecv"].at[k - 1], "y", k - 1, y_peer[k]) for k in range(1, chips)]

    r["ctx_grad"][...] = lax.dot_general(
        grad[...], matrix, (((1,), (1,)), ((), ())), preferred_element_type=F32
    ).astype(BF16)
    if todo:
        pass_on(todo.pop(0))

    hidden = resid[own_rows, :].astype(F32) + hs[0]
    for k in range(1, chips):
        to_y[k - 1].wait_recv()
        hidden = hidden + r["yrecv"][k - 1].astype(F32)
    features = hidden.shape[1]
    row_mean = jnp.sum(hidden, axis=1, keepdims=True) / features
    square_mean = jnp.sum(hidden * hidden, axis=1, keepdims=True) / features
    variance = square_mean - row_mean * row_mean
    feat[own_rows, :] = (
        (hidden - row_mean) * lax.rsqrt(variance + EPSILON) * gain[...]
    ).astype(BF16)
    to_feat = remote(feat.at[own_rows], feat.at[own_rows], "feat", 0, core_peer)
    if len(todo) > 1:
        pass_on(todo.pop(0))
    loads[0].wait()
    loads[1].wait()
    to_feat.wait_recv()

    rows_of = feat[...]
    keys = jnp.dot(rows_of, r["key_w_v"][...], preferred_element_type=F32).astype(BF16)
    values = jnp.dot(rows_of, r["value_w_v"][...], preferred_element_type=F32).astype(BF16)
    scale = 1.0 / math.sqrt(HD)
    attended = []
    for lo in range(0, keys.shape[1], HD):
        scores = (
            lax.dot_general(
                cross_q[:, lo : lo + HD],
                keys[:, lo : lo + HD],
                (((1,), (1,)), ((), ())),
                preferred_element_type=F32,
            )
            * scale
        )
        exponent = jnp.exp(scores - jnp.max(scores, axis=1, keepdims=True))
        probs = (exponent / jnp.sum(exponent, axis=1, keepdims=True)).astype(BF16)
        attended.append(
            jnp.dot(probs, values[:, lo : lo + HD], preferred_element_type=F32).astype(BF16)
        )
    attended = jnp.concatenate(attended, axis=1)

    loads[2].wait()
    out_w, wide = r["out_w_v"], query_state.shape[1]

    def term(chip, core):
        at = pl.multiple_of((2 * chip + core) * wide, 128)
        return jnp.dot(attended, out_w[:, pl.ds(at, wide)], preferred_element_type=F32)

    osend, orecv, own = r["osend"], r["orecv"], r["own"]
    to_pair, to_out = {}, {}
    order = list(range(1, chips)) + [0]
    for k in order:
        osend[k] = term(y_pos[k], 1 - c).astype(BF16)
        to_pair[k] = remote(osend.at[k], orecv.at[k], "pair", k, core_peer)
        own[k] = term(y_pos[k], c)
        if k:
            to_pair[k].wait_recv()
            r["o2send"][k - 1] = (own[k] + orecv[k].astype(F32)).astype(BF16)
            to_out[k] = remote(r["o2send"].at[k - 1], r["o2recv"].at[k - 1], "out", k - 1, y_peer[k])

    while todo:
        pass_on(todo.pop(0))
    if fused:
        rs_x[0].wait_recv()
        total = dwf[d] + r["xrecv"][0].astype(F32)
        for k in range(m - 1, 0, -1):
            rs_z[k].wait_recv()
            total = total + r["zrecv"][k - 1].astype(F32)
        r["proj_grad"][...] = total

    to_pair[0].wait_recv()
    result = query_state[...].astype(F32) + own[0] + orecv[0].astype(F32)
    for k in range(1, chips):
        to_out[k].wait_recv()
        result = result + r["o2recv"][k - 1].astype(F32)
    r["cross_out"][...] = result.astype(BF16)

    sends = [to_core, to_feat] + to_y + list(to_pair.values()) + list(to_out.values())
    if fused:
        sends += ag_z[1:] + ag_x + list(rs_x.values()) + list(rs_z.values())
    for copy in sends:
        copy.wait_send()


def on_device(
    n, h, vit_ctx, vit_resid, vit_proj, vit_grad, norm_gain, cross_q, key_w, value_w, out_w, query_state
):
    rows, width = vit_proj.shape[1:]
    fused = rows % 16 == 0 and n % 2 == 0
    tokens, vrows = vit_ctx.shape
    queries, wide = query_state.shape
    m, chips, half = n // 2, h // 2, tokens // 2
    proj = vit_proj[0] if fused else lax.all_gather(vit_proj, "dp", axis=1, tiled=True)[0]

    ins = {
        "ctx": vit_ctx, "resid": vit_resid, "proj": proj, "grad": vit_grad,
        "gain": norm_gain[None], "cross_q": cross_q, "query_state": query_state,
    }
    streamed = {"key_w": key_w, "value_w": value_w, "out_w": out_w}
    outs = {"ctx_grad": ((tokens, vrows), BF16), "cross_out": ((queries, wide), BF16)}
    dma = lambda count: pltpu.SemaphoreType.DMA((max(count, 1),))
    scratch = {name + "_v": pltpu.VMEM(a.shape, a.dtype) for name, a in streamed.items()}
    scratch |= {
        "load": dma(3),
        "hs": pltpu.VMEM((2, half, width), F32),
        "crecv": pltpu.VMEM((half, width), F32),
        "ysend": pltpu.VMEM((half, width), BF16),
        "yrecv": pltpu.VMEM((max(chips - 1, 1), half, width), BF16),
        "feat": pltpu.VMEM((tokens, width), BF16),
        "osend": pltpu.VMEM((chips, queries, wide), BF16),
        "orecv": pltpu.VMEM((chips, queries, wide), BF16),
        "own": pltpu.VMEM((chips, queries, wide), F32),
        "o2send": pltpu.VMEM((max(chips - 1, 1), queries, wide), BF16),
        "o2recv": pltpu.VMEM((max(chips - 1, 1), queries, wide), BF16),
    }
    sems = {"core": 1, "y": chips - 1, "feat": 1, "pair": chips, "out": chips - 1}
    if fused:
        outs["proj_grad"] = ((rows, width), F32)
        scratch |= {
            "gath": pltpu.VMEM((n, rows, width), BF16),
            "dwf": pltpu.VMEM((n, rows, width), F32),
            "dwb": pltpu.VMEM((m, rows, width), BF16),
            "xrecv": pltpu.VMEM((m, rows, width), BF16),
            "zsend": pltpu.VMEM((max(m - 1, 1), rows, width), BF16),
            "zrecv": pltpu.VMEM((max(m - 1, 1), rows, width), BF16),
        }
        sems |= {"ag_z": m - 1, "ag_x": m, "rs_x": m, "rs_z": m - 1}
    for name, count in sems.items():
        scratch |= {name + "_s": dma(count), name + "_r": dma(count)}

    names = list(ins) + list(streamed) + list(outs) + list(scratch)
    vmem = pl.BlockSpec(memory_space=pltpu.VMEM)
    results = pl.pallas_call(
        functools.partial(kernel, names, n, h, fused),
        out_shape=[jax.ShapeDtypeStruct(*v) for v in outs.values()],
        in_specs=[vmem] * len(ins) + [pl.BlockSpec(memory_space=pl.ANY)] * len(streamed),
        out_specs=[vmem] * len(outs),
        scratch_shapes=list(scratch.values()),
        compiler_params=pltpu.CompilerParams(collective_id=0, has_side_effects=True),
    )(*ins.values(), *streamed.values())
    results = dict(zip(outs, results))
    if fused:
        proj_grad = results["proj_grad"]
    else:
        proj_grad = lax.psum_scatter(
            lax.dot_general(vit_ctx, vit_grad, (((0,), (0,)), ((), ())), preferred_element_type=F32),
            "dp", scatter_dimension=0, tiled=True,
        )
    return (results["ctx_grad"], proj_grad[None], results["cross_out"][None])


def solution(mesh):
    return jax.shard_map(
        functools.partial(on_device, mesh.shape["dp"], mesh.shape["head"]),
        mesh=mesh,
        in_specs=(
            P("dp", "head"),
            P("dp", None),
            P("head", "dp", None),
            P("dp", None),
            P(),
            P(None, "head"),
            P(None, "head"),
            P(None, "head"),
            P("head", None),
            P(None, "head"),
        ),
        out_specs=(P("dp", "head"), P("head", "dp", None), P("dp", None, "head")),
        check_vma=False,
    )
```

time: 205 us -> 60.9 us (0.30)
  waiting for transfers between devices: 174 us -> 0 us
  Pallas kernels: 0 us -> 49.8 us
  between operations: 13.9 us -> 0.64 us
  matrix products: 11.8 us -> 0 us
  local copies, waits for them, and re-layouts: 1.99 us -> 10.1 us
  other arithmetic: 3.64 us -> 0 us
    reduce_scatter x2 -> x0, waiting for transfers between devices: 92.2 us -> none  [the longest x1 73.4 us: on_device(): lax.psum_scatter(lax.dot_general(ctx_part, vit_grad, (((0,), (0,)), ((),...]
    pallas_call x0 -> x1, Pallas kernels: none -> 49.8 us  [on_device(): pl.pallas_call(functools.partial(kernel, names, n, h, fused), out_shape=[...]
    all_gather x1 -> x0, waiting for transfers between devices: 46.6 us -> none  [on_device(): lax.all_gather(vit_proj, 'dp', axis=1, tiled=True)[0]]
    psum x1 -> x0, waiting for transfers between devices: 34.2 us -> none  [on_device(): summed = lax.psum(partial_value, 'head')]
    dot_general x8 -> x0, matrix products: 11.8 us -> none  [the longest x1 3.92 us: on_device(): out_partial = jnp.dot(attended, out_w, preferred_element_type=jnp.float32)]
    unnamed x20 -> x5, local copies, waits for them, and re-layouts: 1.99 us -> 8.81 us
  transfers between devices with their start and end apart: 4 -> 0, of which waited for: 4 -> 0; matrix products, arithmetic and copies ran while one was open for 2% -> 0% of each run, Pallas kernels for 0% -> 0%
where the time goes in v1:
time: 60.9 us; the launch traced here: 60.6 us
  Pallas kernels  49.8 us (82%)
  local copies, waits for them, and re-layouts  10.1 us (17%)
  between operations  0.64 us (1%)
    pallas_call x1, Pallas kernels, on_device(): pl.pallas_call(functools.partial(kernel, names, n, h, fused), out_shape=[...  49.8 us
    unnamed x5, local copies, waits for them, and re-layouts  8.81 us
    broadcast_in_dim x1, local copies, waits for them, and re-layouts, on_device(): norm_gain[None]  1.3 us

profile of v1, /device:TPU:0, one launch (start us, length us, event | category | flops | bytes accessed | tf_op | source)
XLA Modules:
  0.0 60.6 jit_solution(10531277188898853986)
XLA Ops:
  0.6 1.3 %broadcast_in_dim.9.refs_4_ = f32[1,1600]{1,0:T(1,128)} reshape(f32[1600]{0:T(1024)} %param.14) | data formatting | bytes 12800 | tf_op jit(solution)/shard_map/broadcast_in_dim | solution.py:219
  1.9 2.0 %copy.13.refs_1_ = bf16[128,1600]{1,0:T(8,128)(2,1)} copy(bf16[128,1600]{0,1:T(8,128)(2,1)} %param.11) | data formatting | bytes 819200 | tf_op args[1]
  3.9 2.0 %copy.14.refs_3_ = bf16[128,1600]{1,0:T(8,128)(2,1)} copy(bf16[128,1600]{0,1:T(8,128)(2,1)} %param.13) | data formatting | bytes 819200 | tf_op args[3]
  5.9 49.8 %shard_map.121 = (bf16[128,384]{1,0:T(8,128)(2,1)}, bf16[96,1024]{1,0:T(8,128)(2,1)}, f32[48,1600]{1,0:T(8,128)}) custom-call(bf16[128,384]{1,0:T(8,128)(2,1)} %refs_0_.1, bf16[128,1600]{1,0:T(8,128)(2,1)} %copy.13.refs_1_, bf16[48,1600]{1,0:T(8,128)(2,1)} %bitcast.5, bf16[128,1600]{1,0:T(8,128)(2,1)} %copy.14.refs_3_, f32[1,1600]{1,0:T(1,128)} %broadcast_in_dim.9.refs_4_, ...), custom_call_target="tpu_custom_call" | custom-call | tf_op jit(solution)/shard_map/pallas_call | solution.py:255
  55.7 1.5 %copy.18 = bf16[128,384]{1,0:T(8,128)(2,1)} copy(bf16[128,384]{1,0:T(8,128)(2,1)} %get-tuple-element.12) | data formatting | bytes 196608
  57.2 1.7 %copy.19 = f32[1,48,1600]{2,1,0:T(8,128)} copy(f32[1,48,1600]{2,1,0:T(8,128)} %bitcast.3) | data formatting | bytes 614400
  59.0 1.6 %copy.20 = bf16[1,96,1024]{2,1,0:T(8,128)(2,1)} copy(bf16[1,96,1024]{2,1,0:T(8,128)(2,1)} %bitcast.4) | data formatting | bytes 393216

commit v2 on v1

--- a/solution.py
+++ b/solution.py
@@ -26,8 +26,8 @@
     return at
 
 
-def kernel(names, n, h, fused, *refs):
-    r = dict(zip(names, refs))
+def kernel(names, n, h, fused, spans, *refs):
+    r = dict(zip(names, refs), spans=spans)
     ctx, resid, proj, grad, gain, cross_q, query_state = (
         r[k] for k in ("ctx", "resid", "proj", "grad", "gain", "cross_q", "query_state")
     )
@@ -66,72 +66,121 @@
         pl.semaphore_signal(barrier, inc=1, device_id=device, device_id_type=MESH)
     pl.semaphore_wait(barrier, len(greet))
 
+    spans = r["spans"]
+    width = spans[-1][1]
+
+    def flip(src, dst):
+        for lo in range(0, width, 128):
+            hi = min(lo + 128, width)
+            dst[:, lo:hi] = src[lo:hi, :].T
+
     if fused:
         rows = proj.shape[0]
-        width = proj.shape[1]
-        gath, dwf, dwb = r["gath"], r["dwf"], r["dwb"]
-        ag_z = [None] + [remote(proj, gath.at[d], "ag_z", k - 1, z_peer[k]) for k in range(1, m)]
-        ag_x = [remote(proj, gath.at[d], "ag_x", 0, x_peer)]
-        gath[d] = proj[...]
+        dwf, dwb = r["dwf"], r["dwb"]
+        ag_z, ag_x = {}, {}
+        for i, (lo, hi) in enumerate(spans):
+            piece, gath = proj.at[:, lo:hi], r[f"gath{i}"]
+            ag_x[i, 0] = remote(piece, gath.at[d], f"ag_x{i}", 0, x_peer)
+            for k in range(1, m):
+                ag_z[i, k] = remote(piece, gath.at[d], f"ag_z{i}", k - 1, z_peer[k])
+            gath[d] = piece[...]
         ctx_t = ctx[...].T
         for lo in range(0, width, 256):
             hi = min(lo + 256, width)
-            part = jnp.dot(ctx_t, grad[:, lo:hi], preferred_element_type=F32)
+            part = lax.dot_general(
+                ctx_t, grad[lo:hi, :], (((1,), (1,)), ((), ())), preferred_element_type=F32
+            )
             dwf[:, :, lo:hi] = part.reshape(n, rows, hi - lo)
         for k in range(m):
             dwb[k] = dwf[2 * z_pos[k] + 1 - x].astype(BF16)
-        for k in range(1, m):
-            ag_z[k].wait_recv()
-            owner = 2 * z_pos[k] + x
-            ag_x.append(remote(gath.at[owner], gath.at[owner], "ag_x", k, x_peer))
-        rs_x = {}
-        for k in list(range(m - 1, 0, -1)) + [0]:
-            rs_x[k] = remote(dwb.at[k], r["xrecv"].at[k], "rs_x", k, x_peer)
-        rs_z = {}
-
-        def pass_on(k):
-            rs_x[k].wait_recv()
-            r["zsend"][k - 1] = (dwf[2 * z_pos[k] + x] + r["xrecv"][k].astype(F32)).astype(BF16)
-            rs_z[k] = remote(r["zsend"].at[k - 1], r["zrecv"].at[k - 1], "rs_z", k - 1, z_peer[k])
-
-        for k in range(m):
-            ag_x[k].wait_recv()
-        matrix = gath[...].reshape(n * rows, width)
-        todo = list(range(m - 1, 0, -1))
-    else:
-        matrix = proj[...]
-        todo = []
+    flip(grad, r["grad_n"])
+    flip(resid, r["resid_n"])
+    grad, resid = r["grad_n"], r["resid_n"]
 
     half = ctx.shape[0] // 2
     own_rows = pl.ds(pl.multiple_of(c * half, half), half)
     peer_rows = pl.ds(pl.multiple_of((1 - c) * half, half), half)
-    hs, feat = r["hs"], r["feat"]
-    hs[1] = jnp.dot(ctx[peer_rows, :], matrix, preferred_element_type=F32)
-    to_core = remote(hs.at[1], r["crecv"], "core", 0, core_peer)
-    hs[0] = jnp.dot(ctx[own_rows, :], matrix, preferred_element_type=F32)
-    to_core.wait_recv()
-    chip_sum = hs[0] + r["crecv"][...]
-    hs[0] = chip_sum
-    r["ysend"][...] = chip_sum.astype(BF16)
-    to_y = [remote(r["ysend"], r["yrecv"].at[k - 1], "y", k - 1, y_peer[k]) for k in range(1, chips)]
-
-    r["ctx_grad"][...] = lax.dot_general(
-        grad[...], matrix, (((1,), (1,)), ((), ())), preferred_element_type=F32
-    ).astype(BF16)
+    feat = r["feat"]
+    to_core, to_y, rs_x, rs_z = {}, {}, {}, {}
+
+    def forward(i, k):
+        ag_z[i, k].wait_recv()
+        here = r[f"gath{i}"].at[2 * z_pos[k] + x]
+        ag_x[i, k] = remote(here, here, f"ag_x{i}", k, x_peer)
+
+    def matrix(i):
+        lo, hi = spans[i]
+        return r[f"gath{i}"][...].reshape(n * rows, hi - lo) if fused else proj[:, lo:hi]
+
+    def product(i):
+        if fused:
+            for k in range(m):
+                ag_x[i, k].wait_recv()
+        hs = r[f"hs{i}"]
+        hs[1] = jnp.dot(ctx[peer_rows, :], matrix(i), preferred_element_type=F32)
+        to_core[i] = remote(hs.at[1], r[f"crecv{i}"], f"core{i}", 0, core_peer)
+        hs[0] = jnp.dot(ctx[own_rows, :], matrix(i), preferred_element_type=F32)
+
+    def exchange(i):
+        hs, ysend, yrecv = r[f"hs{i}"], r[f"ysend{i}"], r[f"yrecv{i}"]
+        to_core[i].wait_recv()
+        chip_sum = hs[0] + r[f"crecv{i}"][...]
+        hs[0] = chip_sum
+        ysend[...] = chip_sum.astype(BF16)
+        for k in range(1, chips):
+            to_y[i, k] = remote(ysend, yrecv.at[k - 1], f"y{i}", k - 1, y_peer[k])
+
+    def pass_on(k):
+        rs_x[k].wait_recv()
+        r["zsend"][k - 1] = (dwf[2 * z_pos[k] + x] + r["xrecv"][k].astype(F32)).astype(BF16)
+        rs_z[k] = remote(r["zsend"].at[k - 1], r["zrecv"].at[k - 1], "rs_z", k - 1, z_peer[k])
+
+    todo = list(range(m - 1, 0, -1)) if fused else []
+    last = len(spans) - 1
+    for i in range(len(spans)):
+        steps = list(range(1, m)) if fused else []
+        if i == 0:
+            for k in steps:
+                forward(i, k)
+        ahead = steps if i < last else []
+        for k in ahead[:1]:
+            forward(i + 1, k)
+        product(i)
+        for k in ahead[1:2]:
+            forward(i + 1, k)
+        exchange(i)
+        for k in ahead[2:]:
+            forward(i + 1, k)
+        if fused and i == max(last - 1, 0):
+            for k in todo + [0]:
+                rs_x[k] = remote(dwb.at[k], r["xrecv"].at[k], "rs_x", k, x_peer)
+
+    grads = 0.0
+    for i, (lo, hi) in enumerate(spans):
+        grads = grads + lax.dot_general(
+            grad[:, lo:hi], matrix(i), (((1,), (1,)), ((), ())), preferred_element_type=F32
+        )
+    r["ctx_grad"][...] = grads.astype(BF16)
     if todo:
         pass_on(todo.pop(0))
 
-    hidden = resid[own_rows, :].astype(F32) + hs[0]
-    for k in range(1, chips):
-        to_y[k - 1].wait_recv()
-        hidden = hidden + r["yrecv"][k - 1].astype(F32)
-    features = hidden.shape[1]
-    row_mean = jnp.sum(hidden, axis=1, keepdims=True) / features
-    square_mean = jnp.sum(hidden * hidden, axis=1, keepdims=True) / features
+    total, squares = 0.0, 0.0
+    for i, (lo, hi) in enumerate(spans):
+        hidden = resid[own_rows, lo:hi].astype(F32) + r[f"hs{i}"][0]
+        for k in range(1, chips):
+            to_y[i, k].wait_recv()
+            hidden = hidden + r[f"yrecv{i}"][k - 1].astype(F32)
+        r[f"hs{i}"][0] = hidden
+        total = total + jnp.sum(hidden, axis=1, keepdims=True)
+        squares = squares + jnp.sum(hidden * hidden, axis=1, keepdims=True)
+    row_mean, square_mean = total / width, squares / width
     variance = square_mean - row_mean * row_mean
-    feat[own_rows, :] = (
-        (hidden - row_mean) * lax.rsqrt(variance + EPSILON) * gain[...]
-    ).astype(BF16)
+    inverse = lax.rsqrt(variance + EPSILON)
+    scales = gain[...].reshape(1, width)
+    for i, (lo, hi) in enumerate(spans):
+        feat[own_rows, lo:hi] = (
+            (r[f"hs{i}"][0] - row_mean) * inverse * scales[:, lo:hi]
+        ).astype(BF16)
     to_feat = remote(feat.at[own_rows], feat.at[own_rows], "feat", 0, core_peer)
     if len(todo) > 1:
         pass_on(todo.pop(0))
@@ -197,11 +246,16 @@
         result = result + r["o2recv"][k - 1].astype(F32)
     r["cross_out"][...] = result.astype(BF16)
 
-    sends = [to_core, to_feat] + to_y + list(to_pair.values()) + list(to_out.values())
-    if fused:
-        sends += ag_z[1:] + ag_x + list(rs_x.values()) + list(rs_z.values())
+    groups = [to_core, to_y, to_pair, to_out] + ([ag_z, ag_x, rs_x, rs_z] if fused else [])
+    sends = [to_feat] + [copy for group in groups for copy in group.values()]
     for copy in sends:
         copy.wait_send()
+
+
+def hand_over(*refs):
+    count = len(refs) // 2
+    for src, dst in zip(refs[:count], refs[count:]):
+        dst[...] = src[...]
 
 
 def on_device(
@@ -215,8 +269,8 @@
     proj = vit_proj[0] if fused else lax.all_gather(vit_proj, "dp", axis=1, tiled=True)[0]
 
     ins = {
-        "ctx": vit_ctx, "resid": vit_resid, "proj": proj, "grad": vit_grad,
-        "gain": norm_gain[None], "cross_q": cross_q, "query_state": query_state,
+        "ctx": vit_ctx, "resid": vit_resid.T, "proj": proj, "grad": vit_grad.T,
+        "gain": norm_gain, "cross_q": cross_q, "query_state": query_state,
     }
     streamed = {"key_w": key_w, "value_w": value_w, "out_w": out_w}
     outs = {"ctx_grad": ((tokens, vrows), BF16), "cross_out": ((queries, wide), BF16)}
@@ -224,10 +278,8 @@
     scratch = {name + "_v": pltpu.VMEM(a.shape, a.dtype) for name, a in streamed.items()}
     scratch |= {
         "load": dma(3),
-        "hs": pltpu.VMEM((2, half, width), F32),
-        "crecv": pltpu.VMEM((half, width), F32),
-        "ysend": pltpu.VMEM((half, width), BF16),
-        "yrecv": pltpu.VMEM((max(chips - 1, 1), half, width), BF16),
+        "grad_n": pltpu.VMEM((tokens, width), BF16),
+        "resid_n": pltpu.VMEM((tokens, width), BF16),
         "feat": pltpu.VMEM((tokens, width), BF16),
         "osend": pltpu.VMEM((chips, queries, wide), BF16),
         "orecv": pltpu.VMEM((chips, queries, wide), BF16),
@@ -235,31 +287,49 @@
         "o2send": pltpu.VMEM((max(chips - 1, 1), queries, wide), BF16),
         "o2recv": pltpu.VMEM((max(chips - 1, 1), queries, wide), BF16),
     }
-    sems = {"core": 1, "y": chips - 1, "feat": 1, "pair": chips, "out": chips - 1}
+    middle = -(-width // 256) * 128
+    spans = [(0, middle), (middle, width)]
+    sems = {"feat": 1, "pair": chips, "out": chips - 1}
     if fused:
         outs["proj_grad"] = ((rows, width), F32)
         scratch |= {
-            "gath": pltpu.VMEM((n, rows, width), BF16),
             "dwf": pltpu.VMEM((n, rows, width), F32),
             "dwb": pltpu.VMEM((m, rows, width), BF16),
             "xrecv": pltpu.VMEM((m, rows, width), BF16),
             "zsend": pltpu.VMEM((max(m - 1, 1), rows, width), BF16),
             "zrecv": pltpu.VMEM((max(m - 1, 1), rows, width), BF16),
         }
-        sems |= {"ag_z": m - 1, "ag_x": m, "rs_x": m, "rs_z": m - 1}
+        sems |= {"rs_x": m, "rs_z": m - 1}
+    for i, (lo, hi) in enumerate(spans):
+        scratch |= {
+            f"hs{i}": pltpu.VMEM((2, half, hi - lo), F32),
+            f"crecv{i}": pltpu.VMEM((half, hi - lo), F32),
+            f"ysend{i}": pltpu.VMEM((half, hi - lo), BF16),
+            f"yrecv{i}": pltpu.VMEM((max(chips - 1, 1), half, hi - lo), BF16),
+        }
+        sems |= {f"core{i}": 1, f"y{i}": chips - 1}
+        if fused:
+            scratch[f"gath{i}"] = pltpu.VMEM((n, rows, hi - lo), BF16)
+            sems |= {f"ag_z{i}": m - 1, f"ag_x{i}": m}
     for name, count in sems.items():
         scratch |= {name + "_s": dma(count), name + "_r": dma(count)}
 
     names = list(ins) + list(streamed) + list(outs) + list(scratch)
     vmem = pl.BlockSpec(memory_space=pltpu.VMEM)
     results = pl.pallas_call(
-        functools.partial(kernel, names, n, h, fused),
+        functools.partial(kernel, names, n, h, fused, spans),
         out_shape=[jax.ShapeDtypeStruct(*v) for v in outs.values()],
         in_specs=[vmem] * len(ins) + [pl.BlockSpec(memory_space=pl.ANY)] * len(streamed),
         out_specs=[vmem] * len(outs),
         scratch_shapes=list(scratch.values()),
         compiler_params=pltpu.CompilerParams(collective_id=0, has_side_effects=True),
     )(*ins.values(), *streamed.values())
+    results = pl.pallas_call(
+        hand_over,
+        out_shape=[jax.ShapeDtypeStruct(*v) for v in outs.values()],
+        in_specs=[vmem] * len(outs),
+        out_specs=[vmem] * len(outs),
+    )(*results)
     results = dict(zip(outs, results))
     if fused:
         proj_grad = results["proj_grad"]

time: 60.9 us -> 52.3 us (0.86)
  local copies, waits for them, and re-layouts: 10.1 us -> 0 us
  Pallas kernels: 49.8 us -> 51.5 us
    unnamed x5 -> x0, local copies, waits for them, and re-layouts: 8.81 us -> none
    pallas_call x1 -> x2, Pallas kernels: 49.8 us -> 51.5 us  [the longest x1 49.6 us: on_device(): pl.pallas_call(functools.partial(kernel, names, n, h, fused, spans), out_...]
    broadcast_in_dim x1 -> x0, local copies, waits for them, and re-layouts: 1.3 us -> none  [on_device(): norm_gain[None]]
where the time goes in v2:
time: 52.3 us; the launch traced here: 52.2 us
  Pallas kernels  51.5 us (98%)
  between operations  0.64 us (1%)
    pallas_call x1, Pallas kernels, on_device(): pl.pallas_call(functools.partial(kernel, names, n, h, fused, spans), out_...  49.6 us
    pallas_call x1, Pallas kernels, on_device(): pl.pallas_call(hand_over, out_shape=[jax.ShapeDtypeStruct(*v) for v in ou...  1.96 us

profile of v2, /device:TPU:0, one launch (start us, length us, event | category | flops | bytes accessed | tf_op | source)
XLA Modules:
  0.0 52.2 jit_solution(15429527615448116019)
XLA Ops:
  0.6 49.6 %shard_map.121 = (bf16[128,384]{1,0:T(8,128)(2,1)}, bf16[96,1024]{1,0:T(8,128)(2,1)}, f32[48,1600]{1,0:T(8,128)}) custom-call(bf16[128,384]{1,0:T(8,128)(2,1)} %refs_0_.1, bf16[1600,128]{1,0:T(8,128)(2,1)} %bitcast.5, bf16[48,1600]{1,0:T(8,128)(2,1)} %bitcast.7, bf16[1600,128]{1,0:T(8,128)(2,1)} %bitcast.6, f32[1600]{0:T(1024)} %refs_4_.1, ...), custom_call_target="tpu_custom_call" | custom-call | tf_op jit(solution)/shard_map/pallas_call | solution.py:319
  50.2 2.0 %shard_map.122 = (bf16[128,384]{1,0:T(8,128)(2,1)}, bf16[96,1024]{1,0:T(8,128)(2,1)}, f32[48,1600]{1,0:T(8,128)}) custom-call(bf16[128,384]{1,0:T(8,128)(2,1)} %get-tuple-element.9.refs_0_, bf16[96,1024]{1,0:T(8,128)(2,1)} %get-tuple-element.10.refs_1_, f32[48,1600]{1,0:T(8,128)} %get-tuple-element.11.refs_2_), custom_call_target="tpu_custom_call" | custom-call | tf_op jit(solution)/shard_map/pallas_call | solution.py:327

commit v3 on v2

--- a/solution.py
+++ b/solution.py
@@ -26,11 +26,12 @@
     return at
 
 
-def kernel(names, n, h, fused, spans, *refs):
-    r = dict(zip(names, refs), spans=spans)
-    ctx, resid, proj, grad, gain, cross_q, query_state = (
-        r[k] for k in ("ctx", "resid", "proj", "grad", "gain", "cross_q", "query_state")
+def kernel(names, n, h, fused, spans, streams, *refs):
+    r = dict(zip(names, refs), spans=spans, streams=streams)
+    ctx, resid, grad, gain, cross_q, query_state = (
+        r[k + "_v"] for k in ("ctx", "resid", "grad", "gain", "cross_q", "query_state")
     )
+    proj = r["proj"]
     d, e = lax.axis_index("dp"), lax.axis_index("head")
     m, chips = n // 2, h // 2
     z, x = d // 2, lax.rem(d, 2)
@@ -55,10 +56,11 @@
         return copy
 
     loads = []
-    for i, name in enumerate(("key_w", "value_w", "out_w")):
+    for i, name in enumerate(r["streams"]):
         load = pltpu.make_async_copy(r[name], r[name + "_v"], r["load"].at[i])
         load.start()
         loads.append(load)
+    waits = dict(zip(r["streams"], loads))
 
     greet = ([x_peer] + z_peer[1:] if fused else []) + [core_peer] + y_peer[1:]
     barrier = pltpu.get_barrier_semaphore()
@@ -84,6 +86,8 @@
             for k in range(1, m):
                 ag_z[i, k] = remote(piece, gath.at[d], f"ag_z{i}", k - 1, z_peer[k])
             gath[d] = piece[...]
+        waits["ctx"].wait()
+        waits["grad"].wait()
         ctx_t = ctx[...].T
         for lo in range(0, width, 256):
             hi = min(lo + 256, width)
@@ -93,7 +97,14 @@
             dwf[:, :, lo:hi] = part.reshape(n, rows, hi - lo)
         for k in range(m):
             dwb[k] = dwf[2 * z_pos[k] + 1 - x].astype(BF16)
+        early = [m - 1]
+        rs_x = {k: remote(dwb.at[k], r["xrecv"].at[k], "rs_x", k, x_peer) for k in early}
+    else:
+        rs_x = {}
+        waits["ctx"].wait()
+        waits["grad"].wait()
     flip(grad, r["grad_n"])
+    waits["resid"].wait()
     flip(resid, r["resid_n"])
     grad, resid = r["grad_n"], r["resid_n"]
 
@@ -101,7 +112,7 @@
     own_rows = pl.ds(pl.multiple_of(c * half, half), half)
     peer_rows = pl.ds(pl.multiple_of((1 - c) * half, half), half)
     feat = r["feat"]
-    to_core, to_y, rs_x, rs_z = {}, {}, {}, {}
+    to_core, to_y, rs_z = {}, {}, {}
 
     def forward(i, k):
         ag_z[i, k].wait_recv()
@@ -152,8 +163,10 @@
         for k in ahead[2:]:
             forward(i + 1, k)
         if fused and i == max(last - 1, 0):
-            for k in todo + [0]:
+            for k in [k for k in todo + [0] if k not in rs_x]:
                 rs_x[k] = remote(dwb.at[k], r["xrecv"].at[k], "rs_x", k, x_peer)
+            for _ in todo[:1]:
+                pass_on(todo.pop(0))
 
     grads = 0.0
     for i, (lo, hi) in enumerate(spans):
@@ -176,6 +189,7 @@
     row_mean, square_mean = total / width, squares / width
     variance = square_mean - row_mean * row_mean
     inverse = lax.rsqrt(variance + EPSILON)
+    waits["gain"].wait()
     scales = gain[...].reshape(1, width)
     for i, (lo, hi) in enumerate(spans):
         feat[own_rows, lo:hi] = (
@@ -184,13 +198,15 @@
     to_feat = remote(feat.at[own_rows], feat.at[own_rows], "feat", 0, core_peer)
     if len(todo) > 1:
         pass_on(todo.pop(0))
-    loads[0].wait()
-    loads[1].wait()
+    for name in ("key_w", "value_w", "cross_q"):
+        waits[name].wait()
     to_feat.wait_recv()
 
     rows_of = feat[...]
     keys = jnp.dot(rows_of, r["key_w_v"][...], preferred_element_type=F32).astype(BF16)
     values = jnp.dot(rows_of, r["value_w_v"][...], preferred_element_type=F32).astype(BF16)
+    while todo:
+        pass_on(todo.pop(0))
     scale = 1.0 / math.sqrt(HD)
     attended = []
     for lo in range(0, keys.shape[1], HD):
@@ -210,7 +226,8 @@
         )
     attended = jnp.concatenate(attended, axis=1)
 
-    loads[2].wait()
+    waits["out_w"].wait()
+    waits["query_state"].wait()
     out_w, wide = r["out_w_v"], query_state.shape[1]
 
     def term(chip, core):
@@ -268,16 +285,16 @@
     m, chips, half = n // 2, h // 2, tokens // 2
     proj = vit_proj[0] if fused else lax.all_gather(vit_proj, "dp", axis=1, tiled=True)[0]
 
-    ins = {
-        "ctx": vit_ctx, "resid": vit_resid.T, "proj": proj, "grad": vit_grad.T,
-        "gain": norm_gain, "cross_q": cross_q, "query_state": query_state,
+    ins = {"proj": proj}
+    streamed = {
+        "ctx": vit_ctx, "grad": vit_grad.T, "resid": vit_resid.T, "key_w": key_w, "value_w": value_w,
+        "gain": norm_gain, "cross_q": cross_q, "query_state": query_state, "out_w": out_w,
     }
-    streamed = {"key_w": key_w, "value_w": value_w, "out_w": out_w}
     outs = {"ctx_grad": ((tokens, vrows), BF16), "cross_out": ((queries, wide), BF16)}
     dma = lambda count: pltpu.SemaphoreType.DMA((max(count, 1),))
     scratch = {name + "_v": pltpu.VMEM(a.shape, a.dtype) for name, a in streamed.items()}
     scratch |= {
-        "load": dma(3),
+        "load": dma(len(streamed)),
         "grad_n": pltpu.VMEM((tokens, width), BF16),
         "resid_n": pltpu.VMEM((tokens, width), BF16),
         "feat": pltpu.VMEM((tokens, width), BF16),
@@ -317,7 +334,7 @@
     names = list(ins) + list(streamed) + list(outs) + list(scratch)
     vmem = pl.BlockSpec(memory_space=pltpu.VMEM)
     results = pl.pallas_call(
-        functools.partial(kernel, names, n, h, fused, spans),
+        functools.partial(kernel, names, n, h, fused, spans, list(streamed)),
         out_shape=[jax.ShapeDtypeStruct(*v) for v in outs.values()],
         in_specs=[vmem] * len(ins) + [pl.BlockSpec(memory_space=pl.ANY)] * len(streamed),
         out_specs=[vmem] * len(outs),

time: 52.3 us -> 47.2 us (0.902)
  Pallas kernels: 51.5 us -> 46.4 us
    pallas_call x1, Pallas kernels: 49.6 us -> 44.5 us  [on_device(): pl.pallas_call(functools.partial(kernel, names, n, h, fused, spans, list(...]
where the time goes in v3:
time: 47.2 us; the launch traced here: 47.1 us
  Pallas kernels  46.4 us (98%)
  between operations  0.64 us (1%)
    pallas_call x1, Pallas kernels, on_device(): pl.pallas_call(functools.partial(kernel, names, n, h, fused, spans, list(...  44.5 us
    pallas_call x1, Pallas kernels, on_device(): pl.pallas_call(hand_over, out_shape=[jax.ShapeDtypeStruct(*v) for v in ou...  1.96 us

profile of v3, /device:TPU:0, one launch (start us, length us, event | category | flops | bytes accessed | tf_op | source)
XLA Modules:
  0.0 47.1 jit_solution(8504718956064822731)
XLA Ops:
  0.6 44.5 %shard_map.121 = (bf16[128,384]{1,0:T(8,128)(2,1)}, bf16[96,1024]{1,0:T(8,128)(2,1)}, f32[48,1600]{1,0:T(8,128)}) custom-call(bf16[48,1600]{1,0:T(8,128)(2,1)} %bitcast.7, bf16[128,384]{1,0:T(8,128)(2,1)} %refs_1_.1, bf16[1600,128]{1,0:T(8,128)(2,1)} %bitcast.5, bf16[1600,128]{1,0:T(8,128)(2,1)} %bitcast.6, bf16[1600,512]{1,0:T(8,128)(2,1)} %refs_4_.1, ...), custom_call_target="tpu_custom_call" | custom-call | tf_op jit(solution)/shard_map/pallas_call | solution.py:336
  45.1 2.0 %shard_map.122 = (bf16[128,384]{1,0:T(8,128)(2,1)}, bf16[96,1024]{1,0:T(8,128)(2,1)}, f32[48,1600]{1,0:T(8,128)}) custom-call(bf16[128,384]{1,0:T(8,128)(2,1)} %get-tuple-element.9.refs_0_, bf16[96,1024]{1,0:T(8,128)(2,1)} %get-tuple-element.10.refs_1_, f32[48,1600]{1,0:T(8,128)} %get-tuple-element.11.refs_2_), custom_call_target="tpu_custom_call" | custom-call | tf_op jit(solution)/shard_map/pallas_call | solution.py:344
